TPU v7x, 32 devices: a whole 2x2x4 slice. The times are simulated.
32 devices in a mesh: fsdp: 8 (over z, x), tensor: 4 (over y, core).
Axes of the slice: x: 2, y: 2, z: 4, core: 2. Of those that a mesh axis runs over, the one named last changes fastest.
Arguments:
- inputs: bfloat16 [16384, 1024], P(('fsdp', 'tensor')), may hold values from -6 to 6
- segments: int32 [16384], P('fsdp'), may hold values from 0 to 303, as said below
- cotangent: bfloat16 [16384, 1024], P(('fsdp', 'tensor')), may hold values from -6 to 6
- attention_gain: float32 [1024], P(('fsdp', 'tensor')), may hold values from 0.5 to 1.5
- attention_shift: float32 [1024], P(('fsdp', 'tensor')), may hold values from -1.8 to 1.8
- feedforward_gain: float32 [1024], P(('fsdp', 'tensor')), may hold values from 0.5 to 1.5
- feedforward_shift: float32 [1024], P(('fsdp', 'tensor')), may hold values from -1.8 to 1.8
- project_weight: bfloat16 [1024, 3072], P('fsdp', 'tensor'), may hold values from -0.1875 to 0.1875
- project_bias: bfloat16 [3072], P(('tensor', 'fsdp')), may hold values from -3 to 3
- dense_weight: bfloat16 [1024, 1024], P(('tensor', 'fsdp')), may hold values from -0.75 to 0.75
- dense_bias: float32 [1024], P(('fsdp', 'tensor')), may hold values from -1.8 to 1.8
- expand_weight: bfloat16 [1024, 4096], P('fsdp', 'tensor'), may hold values from -0.1875 to 0.1875
- expand_bias: bfloat16 [4096], P(('tensor', 'fsdp')), may hold values from -3 to 3
- shrink_weight: bfloat16 [4096, 1024], P(('tensor', 'fsdp')), may hold values from -0.09375 to 0.09375
- shrink_bias: float32 [1024], P(('fsdp', 'tensor')), may hold values from -1.8 to 1.8
Outputs:
- output: bfloat16 [16384, 1024], P(('fsdp', 'tensor'))
- inputs_gradient: bfloat16 [16384, 1024], P(('fsdp', 'tensor'))
- attention_gain_gradient: float32 [1024], P(('fsdp', 'tensor'))
- attention_shift_gradient: float32 [1024], P(('fsdp', 'tensor'))
- feedforward_gain_gradient: float32 [1024], P(('fsdp', 'tensor'))
- feedforward_shift_gradient: float32 [1024], P(('fsdp', 'tensor'))
- project_weight_gradient: float32 [1024, 3072], P('fsdp', 'tensor')
- project_bias_gradient: float32 [3072], P(('tensor', 'fsdp'))
- dense_weight_gradient: float32 [1024, 1024], P(('tensor', 'fsdp'))
- dense_bias_gradient: float32 [1024], P(('fsdp', 'tensor'))
- expand_weight_gradient: float32 [1024, 4096], P('fsdp', 'tensor')
- expand_bias_gradient: float32 [4096], P(('tensor', 'fsdp'))
- shrink_weight_gradient: float32 [4096, 1024], P(('tensor', 'fsdp'))
- shrink_bias_gradient: float32 [1024], P(('fsdp', 'tensor'))
Inputs may be any that keep to these rules, and one draw needn't show every extreme that they name: `segments`: within each aligned run of 1024 tokens (one sequence) the nonzero segment numbers never fall and occur in no other run; 0 marks padding, which stands only at the end of a run.
All inputs are finite; a program needn't handle non-finite values.
Results may differ from a plain program's by a relative error of at most 0.012.
Values may be sent and summed in bfloat16 or wider, within the bound.
No kernel may reach another device: no remote copies, remote signals or barrier semaphores. Data moves between devices by JAX's collectives and lax.ppermute only.
A program may use at most 192 MiB of HBM per device.

v0:
```python
from functools import partial
import math
import jax
import jax.numpy as jnp
from jax import lax
from jax.sharding import PartitionSpec as P

HD = 64
ROT = 16
SEQ_LEN = 1024
EPS = 1e-05
NEGATIVE = -1e30


def layer_norm(values, gain, shift):
    centre = values - jnp.mean(values, axis=-1, keepdims=True)
    spread = jnp.mean(centre * centre, axis=-1, keepdims=True)
    return centre * lax.rsqrt(spread + EPS) * gain + shift


def rotary_tables(positions):
    half = ROT // 2
    rates = jnp.exp(
        jnp.arange(half, dtype=jnp.int32).astype(jnp.float32) * (-2.0 * math.log(10000.0) / ROT)
    )
    angles = positions.astype(jnp.float32)[:, None] * rates[None, :]
    cosine = jnp.concatenate([jnp.cos(angles), jnp.cos(angles)], axis=1)[:, None, :]
    sine = jnp.concatenate([jnp.sin(angles), jnp.sin(angles)], axis=1)[:, None, :]
    return (cosine, sine)


def rotate(vectors, cosine, sine):
    half = ROT // 2
    turned = vectors[..., :ROT]
    swapped = jnp.concatenate([-turned[..., half:], turned[..., :half]], axis=-1)
    return jnp.concatenate([turned * cosine + swapped * sine, vectors[..., ROT:]], axis=-1)


def rotate_back(grads, cosine, sine):
    half = ROT // 2
    turned = grads[..., :ROT]
    scaled = turned * sine
    backward = jnp.concatenate([scaled[..., half:], -scaled[..., :half]], axis=-1)
    return jnp.concatenate([turned * cosine + backward, grads[..., ROT:]], axis=-1)


def allowed_mask(query_labels, key_labels, query_start):
    query_index = query_start + jnp.arange(query_labels.shape[0], dtype=jnp.int32)
    key_index = jnp.arange(key_labels.shape[0], dtype=jnp.int32)
    causal = key_index[None, :] <= query_index[:, None]
    same = query_labels[:, None] == key_labels[None, :]
    alone = (query_labels[:, None] != 0) | (key_index[None, :] == query_index[:, None])
    return causal & same & alone


def block_scores(query_block, keys, labels, start):
    scale = 1.0 / math.sqrt(HD)
    scores = (
        jnp.einsum("qhd,khd->hqk", query_block, keys, preferred_element_type=jnp.float32) * scale
    )
    mask = allowed_mask(labels[start : start + query_block.shape[0]], labels, start)
    return jnp.where(mask[None], scores, NEGATIVE)


def attend_sequence(items):
    query, keys, values, labels = items
    length = keys.shape[0]
    rows_block = min(512, length)
    outputs = []
    totals = []
    for block in range(length // rows_block):
        start = block * rows_block
        scores = block_scores(query[start : start + rows_block], keys, labels, start)
        top = jnp.max(scores, axis=-1, keepdims=True)
        probs = jnp.exp(scores - top)
        total = jnp.sum(probs, axis=-1, keepdims=True)
        probs = probs / total
        mixed = jnp.einsum(
            "hqk,khd->qhd", probs.astype(jnp.bfloat16), values, preferred_element_type=jnp.float32
        )
        outputs.append(mixed.astype(jnp.bfloat16))
        totals.append((top + jnp.log(total))[..., 0])
    return (jnp.concatenate(outputs, axis=0), jnp.concatenate(totals, axis=1))


def attend_back(items):
    query, keys, values, labels, totals, grads = items
    scale = 1.0 / math.sqrt(HD)
    length = keys.shape[0]
    rows_block = min(512, length)
    key_grad = jnp.zeros(keys.shape, jnp.float32)
    value_grad = jnp.zeros(values.shape, jnp.float32)
    query_grads = []
    for block in range(length // rows_block):
        start = block * rows_block
        query_block = query[start : start + rows_block]
        grad_block = grads[start : start + rows_block]
        scores = block_scores(query_block, keys, labels, start)
        probs = jnp.exp(scores - totals[:, start : start + rows_block, None])
        probs_grad = jnp.einsum(
            "qhd,khd->hqk", grad_block, values, preferred_element_type=jnp.float32
        )
        inner = jnp.sum(probs * probs_grad, axis=-1, keepdims=True)
        scores_grad = (probs * (probs_grad - inner)).astype(jnp.bfloat16)
        query_grads.append(
            jnp.einsum("hqk,khd->qhd", scores_grad, keys, preferred_element_type=jnp.float32)
            * scale
        )
        key_grad = (
            key_grad
            + jnp.einsum(
                "hqk,qhd->khd", scores_grad, query_block, preferred_element_type=jnp.float32
            )
            * scale
        )
        value_grad = value_grad + jnp.einsum(
            "hqk,qhd->khd",
            probs.astype(jnp.bfloat16),
            grad_block,
            preferred_element_type=jnp.float32,
        )
    return (jnp.concatenate(query_grads, axis=0), key_grad, value_grad)


def contract_rows(left, right):
    return lax.dot_general(
        left, right, (((0,), (0,)), ((), ())), preferred_element_type=jnp.float32
    )


def contract_columns(left, right):
    return lax.dot_general(
        left, right, (((1,), (1,)), ((), ())), preferred_element_type=jnp.float32
    )


def local(
    inputs,
    segments,
    cotangent,
    attention_gain,
    attention_shift,
    feedforward_gain,
    feedforward_shift,
    project_weight,
    project_bias,
    dense_weight,
    dense_bias,
    expand_weight,
    expand_bias,
    shrink_weight,
    shrink_bias,
):
    rank = lax.axis_index("tensor")
    rows = inputs.shape[0]
    group = segments.shape[0]
    count = group // SEQ_LEN
    vectors = (
        lax.all_gather(attention_gain, ("fsdp", "tensor"), axis=0, tiled=True),
        lax.all_gather(attention_shift, ("fsdp", "tensor"), axis=0, tiled=True),
        lax.all_gather(feedforward_gain, ("fsdp", "tensor"), axis=0, tiled=True),
        lax.all_gather(feedforward_shift, ("fsdp", "tensor"), axis=0, tiled=True),
        lax.all_gather(dense_bias, ("fsdp", "tensor"), axis=0, tiled=True),
        lax.all_gather(shrink_bias, ("fsdp", "tensor"), axis=0, tiled=True),
    )
    gain_one, shift_one, gain_two, shift_two, dense_full, shrink_full = vectors
    gathered = (
        lax.all_gather(project_weight, "fsdp", axis=0, tiled=True),
        lax.all_gather(expand_weight, "fsdp", axis=0, tiled=True),
        lax.all_gather(dense_weight, "fsdp", axis=0, tiled=True),
        lax.all_gather(shrink_weight, "fsdp", axis=0, tiled=True),
        lax.all_gather(project_bias, "fsdp", axis=0, tiled=True),
        lax.all_gather(expand_bias, "fsdp", axis=0, tiled=True),
    )
    project_local, expand_local, dense_local, shrink_local, project_offset, expand_offset = gathered
    features = inputs.astype(jnp.float32)
    local_one = layer_norm(features, gain_one, shift_one).astype(jnp.bfloat16)
    local_two = layer_norm(features, gain_two, shift_two).astype(jnp.bfloat16)
    normed_one, normed_two = (
        lax.all_gather(local_one, "tensor", axis=0, tiled=True),
        lax.all_gather(local_two, "tensor", axis=0, tiled=True),
    )
    positions = jnp.arange(group, dtype=jnp.int32) % SEQ_LEN
    cosine, sine = rotary_tables(positions)
    heads = project_local.shape[1] // (3 * HD)
    projected = jnp.dot(
        normed_one, project_local, preferred_element_type=jnp.float32
    ) + project_offset.astype(jnp.float32)
    projected = projected.reshape(group, heads, 3, HD)
    query = rotate(projected[:, :, 0], cosine, sine).astype(jnp.bfloat16)
    keys = rotate(projected[:, :, 1], cosine, sine).astype(jnp.bfloat16)
    values = projected[:, :, 2].astype(jnp.bfloat16)

    def shaped(array):
        return array.reshape((count, SEQ_LEN) + array.shape[1:])

    labels = segments.reshape(count, SEQ_LEN)
    mixed, totals = lax.map(attend_sequence, (shaped(query), shaped(keys), shaped(values), labels))
    mixed = mixed.reshape(group, heads * HD)
    hidden = jnp.dot(
        normed_two, expand_local, preferred_element_type=jnp.float32
    ) + expand_offset.astype(jnp.float32)
    active = jax.nn.gelu(hidden, approximate=False).astype(jnp.bfloat16)
    mixed_rows = lax.slice_in_dim(mixed, 0, rows * lax.axis_size("tensor"), axis=0)
    branch = lax.psum_scatter(
        (
            jnp.dot(mixed_rows, dense_local, preferred_element_type=jnp.float32)
            + jnp.dot(active, shrink_local, preferred_element_type=jnp.float32)
        ).astype(jnp.bfloat16),
        "tensor",
        scatter_dimension=0,
        tiled=True,
    ).astype(jnp.float32)
    output = (features + branch + dense_full + shrink_full).astype(jnp.bfloat16)
    own_labels = lax.dynamic_slice_in_dim(segments, rank * rows, rows, 0)
    upstream = cotangent.astype(jnp.float32) * (own_labels != 0).astype(jnp.float32)[:, None]
    branch_grad = lax.all_gather(upstream.astype(jnp.bfloat16), "tensor", axis=0, tiled=True)
    bias_grad = jnp.sum(upstream, axis=0)
    shrink_grad = contract_rows(active, branch_grad)
    active_grad = contract_columns(branch_grad, shrink_local)
    gelu_value, gelu_pull = jax.vjp(partial(jax.nn.gelu, approximate=False), hidden)
    hidden_grad = gelu_pull(active_grad)[0].astype(jnp.bfloat16)
    expand_grad = contract_rows(normed_two, hidden_grad)
    expand_offset_grad = jnp.sum(hidden_grad.astype(jnp.float32), axis=0)
    normed_two_grad = contract_columns(hidden_grad, expand_local)
    dense_grad = contract_rows(mixed, branch_grad)
    mixed_grad = (
        contract_columns(branch_grad, dense_local).astype(jnp.bfloat16).reshape(group, heads, HD)
    )
    query_grad, key_grad, value_grad = lax.map(
        attend_back,
        (shaped(query), shaped(keys), shaped(values), labels, totals, shaped(mixed_grad)),
    )
    query_grad = rotate_back(query_grad.reshape(group, heads, HD), cosine, sine)
    key_grad = rotate_back(key_grad.reshape(group, heads, HD), cosine, sine)
    projected_grad = jnp.stack([query_grad, key_grad, value_grad.reshape(group, heads, HD)], axis=2)
    projected_grad = projected_grad.reshape(group, 3 * heads * HD).astype(jnp.bfloat16)
    project_grad = contract_rows(normed_one, projected_grad)
    project_offset_grad = jnp.sum(projected_grad.astype(jnp.float32), axis=0)
    normed_one_grad = contract_columns(projected_grad, project_local)
    weight_sums = (
        lax.psum_scatter(project_grad, "fsdp", scatter_dimension=0, tiled=True),
        lax.psum_scatter(expand_grad, "fsdp", scatter_dimension=0, tiled=True),
        lax.psum_scatter(dense_grad, "fsdp", scatter_dimension=0, tiled=True),
        lax.psum_scatter(shrink_grad, "fsdp", scatter_dimension=0, tiled=True),
        lax.psum_scatter(project_offset_grad, "fsdp", scatter_dimension=0, tiled=True),
        lax.psum_scatter(expand_offset_grad, "fsdp", scatter_dimension=0, tiled=True),
    )
    project_sum, expand_sum, dense_sum, shrink_sum, project_offset_sum, expand_offset_sum = (
        weight_sums
    )
    one_rows, two_rows = (
        lax.psum_scatter(
            normed_one_grad.astype(jnp.bfloat16), "tensor", scatter_dimension=0, tiled=True
        ).astype(jnp.float32),
        lax.psum_scatter(
            normed_two_grad.astype(jnp.bfloat16), "tensor", scatter_dimension=0, tiled=True
        ).astype(jnp.float32),
    )
    norm_value, first_pull = jax.vjp(layer_norm, features, gain_one, shift_one)
    first_inputs, first_gain, first_shift = first_pull(one_rows)
    norm_other, second_pull = jax.vjp(layer_norm, features, gain_two, shift_two)
    second_inputs, second_gain, second_shift = second_pull(two_rows)
    inputs_gradient = (upstream + first_inputs + second_inputs).astype(jnp.bfloat16)
    vector_sums = (
        lax.psum_scatter(first_gain, ("fsdp", "tensor"), scatter_dimension=0, tiled=True),
        lax.psum_scatter(first_shift, ("fsdp", "tensor"), scatter_dimension=0, tiled=True),
        lax.psum_scatter(second_gain, ("fsdp", "tensor"), scatter_dimension=0, tiled=True),
        lax.psum_scatter(second_shift, ("fsdp", "tensor"), scatter_dimension=0, tiled=True),
        lax.psum_scatter(bias_grad, ("fsdp", "tensor"), scatter_dimension=0, tiled=True),
    )
    gain_one_sum, shift_one_sum, gain_two_sum, shift_two_sum, bias_sum = vector_sums
    return (
        output,
        inputs_gradient,
        gain_one_sum,
        shift_one_sum,
        gain_two_sum,
        shift_two_sum,
        project_sum,
        project_offset_sum,
        dense_sum,
        bias_sum,
        expand_sum,
        expand_offset_sum,
        shrink_sum,
        bias_sum,
    )


def solution(mesh):
    in_specs = (
        P(("fsdp", "tensor"), None),
        P("fsdp"),
        P(("fsdp", "tensor"), None),
        P(("fsdp", "tensor")),
        P(("fsdp", "tensor")),
        P(("fsdp", "tensor")),
        P(("fsdp", "tensor")),
        P("fsdp", "tensor"),
        P(("tensor", "fsdp")),
        P(("tensor", "fsdp"), None),
        P(("fsdp", "tensor")),
        P("fsdp", "tensor"),
        P(("tensor", "fsdp")),
        P(("tensor", "fsdp"), None),
        P(("fsdp", "tensor")),
    )
    out_specs = (
        P(("fsdp", "tensor"), None),
        P(("fsdp", "tensor"), None),
        P(("fsdp", "tensor")),
        P(("fsdp", "tensor")),
        P(("fsdp", "tensor")),
        P(("fsdp", "tensor")),
        P("fsdp", "tensor"),
        P(("tensor", "fsdp")),
        P(("tensor", "fsdp"), None),
        P(("fsdp", "tensor")),
        P("fsdp", "tensor"),
        P(("tensor", "fsdp")),
        P(("tensor", "fsdp"), None),
        P(("fsdp", "tensor")),
    )
    return jax.shard_map(local, mesh=mesh, in_specs=in_specs, out_specs=out_specs, check_vma=False)
```

profile of v0, /device:TPU:0, one launch (start us, length us, event | category | flops | bytes accessed | tf_op | source)
XLA Modules:
  0.0 900.5 jit_solution(8306996030455223238)
XLA Ops:
  11.4 42.7 %all-reduce.15 = (f32[1024]{0:T(1024)S(1)}, f32[1024]{0:T(1024)S(1)}, f32[1024]{0:T(1024)S(1)}, f32[1024]{0:T(1024)S(1)}) all-reduce(f32[1024]{0:T(1024)S(1)} %dynamic-update-slice.4, f32[1024]{0:T(1024)S(1)} %dynamic-update-slice.3, f32[1024]{0:T(1024)S(1)} %dynamic-update-slice.1, ...), channel_id=1, replica_groups=mesh['fsdp'=8,'tensor'=4] {'fsdp','tensor'}, use_global_device_ids=true, to_apply=%add.4 | all-reduce | flops 4096 | bytes 32768
  57.8 3.2 fusion.108
  66.4 21.0 %all-reduce.2 = bf16[768]{0:T(1024)(128)(2,1)S(1)} all-reduce(bf16[768]{0:T(1024)(128)(2,1)S(1)} %dynamic-update-slice.2), channel_id=1, replica_groups=mesh['fsdp'=8,'tensor'=4] {'fsdp'}, use_global_device_ids=true, to_apply=%add.2 | all-reduce | flops 768 | bytes 3072
  87.3 33.6 %all_gather.50 = bf16[256,1024]{1,0:T(8,128)(2,1)} all-gather(bf16[32,1024]{1,0:T(8,128)(2,1)S(1)} %copy-done.28), channel_id=1, replica_groups=mesh['fsdp'=8,'tensor'=4] {'fsdp'}, dimensions={0}, use_global_device_ids=true | all-gather | bytes 589824 | tf_op jit(solution)/shard_map/all_gather | solution.py:170
  121.4 5.8 convolution_add_fusion.1
  131.3 2.5 pad_maximum_fusion.1
  134.3 2.6 concatenate.55
  142.6 37.2 %while.26 = (s32[]{:T(128)}, bf16[2,1024,4,64]{1,3,2,0:T(8,128)(2,1)}, f32[2,4,1024]{2,1,0:T(4,128)S(1)}, bf16[2,1024,4,64]{1,3,2,0:T(8,128)(2,1)}, s32[2,1024]{...) while((s32[]{:T(128)}, ...), condition=%wide.region_7.8_spmd, body=%wide.region_2.7_spmd.sunk | while | flops 1131677184 | bytes 58922628 | solution.py:198
  146.8 2.3 fusion.211
  150.9 2.3 fusion.208
  153.3 3.6 fusion.212
  156.9 3.6 fusion.209
  165.2 2.3 fusion.211
  171.6 3.6 fusion.212
  175.3 3.6 fusion.209
  179.8 4.5 convolution_convert_fusion.2
  184.3 4.4 reshape.530
  188.7 4.1 copy.57
  192.9 193.4 %while.27 = (s32[]{:T(128)}, f32[2,1024,4,64]{1,0,3,2:T(2,128)}, f32[2,1024,4,64]{1,0,3,2:T(2,128)}, bf16[2,1024,4,64]{1,0,3,2:T(2,128)(2,1)}, bf16[2,1024,4,64]...) while((s32[]{:T(128)}, f32[2,1024,4,64]{1,0,3,2:T(2,128)}, ...), condition=%wide.region_12.13_spmd, body=%wide.region_9.12_spmd.sunk | while | flops 2755130880 | bytes 284876160 | solution.py:230
  196.5 4.6 multiply_reduce_fusion.5
  201.1 2.4 multiply_convert_fusion.6
  205.6 4.6 multiply_reduce_fusion.4
  210.3 2.4 multiply_convert_fusion.5
  215.8 18.7 %dynamic_update_slice.28 = f32[2,1024,4,64]{1,0,3,2:T(2,128)} dynamic-update-slice(f32[2,1024,4,64]{1,0,3,2:T(2,128)} %get-tuple-element.462, f32[1,1024,4,64]{1,0,3,2:T(1,128)S(1)} %copy.97, s32[]{:T(128)} %get-tuple-element.460, s32[]{:T(128)} %constant.44.clone.1..sunk.1, s32[]{:T(128)} %constant.44.clone.1..sunk.1, s32[]{:T(128)} %constant.44.clone.1..sunk.1) | dynamic-update-slice | bytes 2097156 | tf_op jit(solution)/shard_map/while/body/jit(dynamic_update_index_in_dim)/dynamic_update_slice | solution.py:230
  234.5 3.7 fusion.230
  240.8 18.7 %dynamic_update_slice.27 = f32[2,1024,4,64]{1,0,3,2:T(2,128)} dynamic-update-slice(f32[2,1024,4,64]{1,0,3,2:T(2,128)} %get-tuple-element.461, f32[1,1024,4,64]{1,0,3,2:T(1,128)S(1)} %copy.96, s32[]{:T(128)} %get-tuple-element.460, s32[]{:T(128)} %constant.44.clone.1..sunk.1, s32[]{:T(128)} %constant.44.clone.1..sunk.1, s32[]{:T(128)} %constant.44.clone.1..sunk.1) | dynamic-update-slice | bytes 2097156 | tf_op jit(solution)/shard_map/while/body/jit(dynamic_update_index_in_dim)/dynamic_update_slice | solution.py:230
  259.5 5.8 fusion.233
  265.3 5.9 fusion.234
  272.1 17.4 %dynamic_update_slice.29 = bf16[2,1024,4,64]{1,0,3,2:T(2,128)(2,1)} dynamic-update-slice(bf16[2,1024,4,64]{1,0,3,2:T(2,128)(2,1)} %get-tuple-element.463, bf16[1,1024,4,64]{1,0,3,2:T(2,128)(2,1)S(1)} %copy.98, s32[]{:T(128)} %get-tuple-element.460, s32[]{:T(128)} %constant.44.clone.1..sunk.1, s32[]{:T(128)} %constant.44.clone.1..sunk.1, s32[]{:T(128)} %constant.44.clone.1..sunk.1) | dynamic-update-slice | bytes 1048580 | tf_op jit(solution)/shard_map/while/body/jit(dynamic_update_index_in_dim)/dynamic_update_slice | solution.py:230
  292.9 4.6 multiply_reduce_fusion.5
  297.5 2.4 multiply_convert_fusion.6
  302.1 4.6 multiply_reduce_fusion.4
  306.7 2.4 multiply_convert_fusion.5
  312.3 18.7 %dynamic_update_slice.28 = f32[2,1024,4,64]{1,0,3,2:T(2,128)} dynamic-update-slice(f32[2,1024,4,64]{1,0,3,2:T(2,128)} %get-tuple-element.462, f32[1,1024,4,64]{1,0,3,2:T(1,128)S(1)} %copy.97, s32[]{:T(128)} %get-tuple-element.460, s32[]{:T(128)} %constant.44.clone.1..sunk.1, s32[]{:T(128)} %constant.44.clone.1..sunk.1, s32[]{:T(128)} %constant.44.clone.1..sunk.1) | dynamic-update-slice | bytes 2097156 | tf_op jit(solution)/shard_map/while/body/jit(dynamic_update_index_in_dim)/dynamic_update_slice | solution.py:230
  331.0 3.7 fusion.230
  337.3 18.7 %dynamic_update_slice.27 = f32[2,1024,4,64]{1,0,3,2:T(2,128)} dynamic-update-slice(f32[2,1024,4,64]{1,0,3,2:T(2,128)} %get-tuple-element.461, f32[1,1024,4,64]{1,0,3,2:T(1,128)S(1)} %copy.96, s32[]{:T(128)} %get-tuple-element.460, s32[]{:T(128)} %constant.44.clone.1..sunk.1, s32[]{:T(128)} %constant.44.clone.1..sunk.1, s32[]{:T(128)} %constant.44.clone.1..sunk.1) | dynamic-update-slice | bytes 2097156 | tf_op jit(solution)/shard_map/while/body/jit(dynamic_update_index_in_dim)/dynamic_update_slice | solution.py:230
  355.9 5.7 fusion.233
  361.7 5.9 fusion.234
  368.4 17.4 %dynamic_update_slice.29 = bf16[2,1024,4,64]{1,0,3,2:T(2,128)(2,1)} dynamic-update-slice(bf16[2,1024,4,64]{1,0,3,2:T(2,128)(2,1)} %get-tuple-element.463, bf16[1,1024,4,64]{1,0,3,2:T(2,128)(2,1)S(1)} %copy.98, s32[]{:T(128)} %get-tuple-element.460, s32[]{:T(128)} %constant.44.clone.1..sunk.1, s32[]{:T(128)} %constant.44.clone.1..sunk.1, s32[]{:T(128)} %constant.44.clone.1..sunk.1) | dynamic-update-slice | bytes 1048580 | tf_op jit(solution)/shard_map/while/body/jit(dynamic_update_index_in_dim)/dynamic_update_slice | solution.py:230
  386.2 3.1 reshape.508
  389.3 4.0 reshape.509
  394.4 2.4 slice.161
  404.7 5.3 convolution_convert_fusion
  410.6 16.1 %all-gather = bf16[8,1,128]{2,1,0:T(2,128)(2,1)S(1)} all-gather(bf16[1,1,128]{2,1,0:T(2,128)(2,1)S(1)} %bitcast.260), channel_id=1, replica_groups=mesh['fsdp'=8,'tensor'=4] {'fsdp'}, dimensions={0}, use_global_device_ids=true | all-gather | bytes 2304 | tf_op jit(solution)/shard_map/all_gather | solution.py:173
  426.8 10.7 %fusion.139 = f32[2048,1024]{1,0:T(8,128)} fusion(bf16[2048,1024]{1,0:T(8,128)(2,1)} %all-gather.12.cloned.1.call-done, bf16[1024,1024]{1,0:T(8,128)(2,1)} %all-gather.14.cloned.1.call-done), kind=kOutput, calls=%fused_computation.245 | convolution fusion | flops 4294967296 | bytes 14680064 | tf_op jit(solution)/shard_map/dot_general | solution.py:200
  437.5 28.0 %convert_reduce_fusion = (f32[1024]{0:T(1024)S(1)}, bf16[2048,1024]{1,0:T(8,128)(2,1)S(1)}, f32[2048,1024]{1,0:T(8,128)}) fusion(f32[2048,1024]{1,0:T(8,128)} %fusion.139, f32[1024]{0:T(1024)S(1)} %bitcast.258, bf16[2048,1024]{1,0:T(8,128)(2,1)} %all-gather.18.cloned.1.call-done, bf16[1024,1024]{1,0:T(8,128)(2,1)} %all-gather.16.cloned.1.call-done), kind=kOutput, calls=%fused_computation.132 | convolution fusion | flops 4452252672 | bytes 27271168 | tf_op jit(solution)/shard_map/dot_general | solution.py:132
  467.4 6.4 convolution_convert_fusion.1
  476.7 12.3 %multiply_convert_fusion.2 = bf16[2048,1024]{1,0:T(8,128)(2,1)} fusion(f32[2048,1024]{1,0:T(8,128)} %get-tuple-element.214, f32[2048,1024]{1,0:T(8,128)} %fusion.139, f32[1024]{0:T(1024)S(1)} %bitcast.259), kind=kLoop, calls=%fused_computation.135 | loop fusion | flops 8388608 | bytes 20975616 | tf_op jit(solution)/shard_map/convert_element_type | solution.py:203
  489.0 6.4 fusion.140
  495.4 3.3 add_convert_fusion.1
  498.7 4.5 fusion.142
  503.3 8.4 fusion.141
  512.0 10.0 %fusion.144 = f32[1024,1024]{1,0:T(8,128)} fusion(bf16[2048,1024]{1,0:T(8,128)(2,1)} %multiply_convert_fusion.2, bf16[2048,1024]{1,0:T(8,128)(2,1)} %all-gather.18.cloned.1.call-done), kind=kOutput, calls=%fused_computation.250 | convolution fusion | flops 4294967296 | bytes 12582912 | tf_op jit(solution)/shard_map/dot_general | solution.py:126
  522.1 10.5 %fusion.143 = f32[1024,1024]{1,0:T(8,128)} fusion(bf16[2048,1024]{1,0:T(8,128)(2,1)} %all-gather.12.cloned.1.call-done, bf16[2048,1024]{1,0:T(8,128)(2,1)} %copy-done.46), kind=kOutput, calls=%fused_computation.249 | convolution fusion | flops 4294967296 | bytes 12582912 | tf_op jit(solution)/shard_map/dot_general | solution.py:126
  534.8 20.0 %all-reduce.16 = (f32[768]{0:T(1024)S(1)}, f32[1024]{0:T(1024)S(1)}) all-reduce(f32[768]{0:T(1024)S(1)} %reduce_sum.174, f32[1024]{0:T(1024)S(1)} %get-tuple-element.212), channel_id=10, replica_groups=mesh['fsdp'=8,'tensor'=4] {'fsdp'}, use_global_device_ids=true, to_apply=%region_29.30.clone | all-reduce | flops 1792 | bytes 14336
  556.0 2.7 fusion.112
  558.6 3.4 fusion.118
  562.1 2.6 add_convert_fusion.2
  564.6 37.5 %all-reduce.14 = (f32[1024]{0:T(1024)S(1)}, f32[1024]{0:T(1024)S(1)}, f32[1024]{0:T(1024)S(1)}, f32[1024]{0:T(1024)S(1)}, f32[1024]{0:T(1024)S(1)}, /*index=5*/f32[1024]{0:T(1024)S(1)}, f32[1024]{0:T(1024)S(1)}) all-reduce(f32[1024]{0:T(1024)S(1)} %dynamic-update-slice.6, ...), channel_id=1, replica_groups=mesh['fsdp'=8,'tensor'=4] {'fsdp','tensor'}, use_global_device_ids=true, to_apply=%add.6 | all-reduce | flops 7168 | bytes 57344
  604.6 2.6 fusion.116
  607.2 24.7 %reduce-scatter.16.cloned.1.call-done = f32[32,1024]{1,0:T(8,128)} async-done(((f32[256,1024]{1,0:T(8,128)}), f32[32,1024]{1,0:T(8,128)}) %reduce-scatter.16.cloned.1.call-update) | async-done | bytes 131088 | tf_op jit(solution)/shard_map/reduce_scatter | solution.py:244
  631.9 77.4 %reduce-scatter.14.cloned.1.call-done = f32[128,768]{1,0:T(8,128)} async-done(((f32[1024,768]{1,0:T(8,128)}), f32[128,768]{1,0:T(8,128)}) %reduce-scatter.14.cloned.1.call-update) | async-done | bytes 393232 | tf_op jit(solution)/shard_map/reduce_scatter | solution.py:242
  709.3 91.2 %reduce-scatter.20.cloned.1.call-done = f32[128,1024]{1,0:T(8,128)} async-done(((f32[1024,1024]{1,0:T(8,128)}), f32[128,1024]{1,0:T(8,128)}) %reduce-scatter.20.cloned.1.call-update) | async-done | bytes 524304 | tf_op jit(solution)/shard_map/reduce_scatter | solution.py:245
  800.5 92.5 %reduce-scatter.18.cloned.1.call-done = f32[128,1024]{1,0:T(8,128)} async-done(((f32[1024,1024]{1,0:T(8,128)}), f32[128,1024]{1,0:T(8,128)}) %reduce-scatter.18.cloned.1.call-update) | async-done | bytes 524304 | tf_op jit(solution)/shard_map/reduce_scatter | solution.py:243
  (275 shorter events, 81.6 us)
Async XLA Ops:
  7.2 53.9 %copy-start.36 = (s32[2048]{0:T(1024)S(1)}, s32[2048]{0:T(1024)}, u32[]{:S(2)}) copy-start(s32[2048]{0:T(1024)} %param.20) | copy-start | bytes 24580
  7.2 54.6 %copy-start.11 = (bf16[512,1024]{1,0:T(8,128)(2,1)S(1)}, bf16[512,1024]{1,0:T(8,128)(2,1)}, u32[]{:S(2)}) copy-start(bf16[512,1024]{1,0:T(8,128)(2,1)} %param.21) | copy-start | bytes 3145732
  7.2 114.1 %all-gather.10.cloned.1.call-start = ((), (), s32[]{:S(2)}) async-start(), calls=%async_computation.8 | async-start | bytes 1769472 | tf_op jit(solution)/shard_map/all_gather | solution.py:168
  7.9 113.4 %all-gather.8.cloned.1.call-start = ((), (), s32[]{:S(2)}) async-start(), calls=%async_computation.7 | async-start | bytes 5242880 | tf_op jit(solution)/shard_map/all_gather | solution.py:180
  54.1 8.9 copy-start.24
  54.1 8.9 copy-start.26
  55.5 2.2 copy-start.22
  57.2 3.8 copy-start.29
  57.8 7.1 copy-start.37
  57.8 8.4 copy-start.42
  57.8 29.6 %copy-start.28 = (bf16[32,1024]{1,0:T(8,128)(2,1)S(1)}, bf16[32,1024]{1,0:T(8,128)(2,1)}, u32[]{:S(2)}) copy-start(bf16[32,1024]{1,0:T(8,128)(2,1)} %param.28) | copy-start | bytes 196612
  61.0 118.8 %all-gather.18.cloned.1.call-start = ((), (), s32[]{:S(2)}) async-start(), calls=%async_computation.13 | async-start | bytes 5242880 | tf_op jit(solution)/shard_map/all_gather | solution.py:217
  63.0 363.8 %all-gather.14.cloned.1.call-start = ((), (), s32[]{:S(2)}) async-start(), calls=%async_computation.10 | async-start | bytes 2359296 | tf_op jit(solution)/shard_map/all_gather | solution.py:169
  63.6 363.2 %all-gather.12.cloned.1.call-start = ((), (), s32[]{:S(2)}) async-start(), calls=%async_computation.9 | async-start | bytes 5242880 | tf_op jit(solution)/shard_map/all_gather | solution.py:181
  64.2 373.3 %all-gather.16.cloned.1.call-start = ((), (), s32[]{:S(2)}) async-start(), calls=%async_computation.11 | async-start | bytes 2359296 | tf_op jit(solution)/shard_map/all_gather | solution.py:171
  64.7 491.2 %reduce-scatter.10.cloned.1.call-start = ((), (), s32[]{:S(2)}) async-start(), calls=%async_computation.14 | async-start | bytes 5242880 | tf_op jit(solution)/shard_map/reduce_scatter | solution.py:253
  121.3 8.3 copy-start.18
  121.3 8.2 copy-start.20
  142.6 37.2 %copy-start.16 = (bf16[256,1024]{1,0:T(8,128)(2,1)S(1)}, bf16[256,1024]{1,0:T(8,128)(2,1)}, u32[]{:S(2)}) copy-start(bf16[256,1024]{1,0:T(8,128)(2,1)} %all_gather.50) | copy-start | bytes 1572868
  193.0 19.7 %copy-start.5 = (bf16[2,1024,4,64]{1,3,2,0:T(8,128)(2,1)}, bf16[2,1024,4,64]{1,3,2,0:T(8,128)(2,1)S(1)}, u32[]{:S(2)}) copy-start(bf16[2,1024,4,64]{1,3,2,0:T(8,128)(2,1)S(1)} %get-tuple-element.479) | copy-start | bytes 3145732 | tf_op jit(solution)/shard_map/while
  195.1 1.4 copy-start.8
  196.4 4.7 copy-start.1
  203.5 2.2 copy-start.4
  205.6 4.6 copy-start
  212.7 2.1 copy-start.2
  234.5 3.7 copy-start.3
  265.3 24.2 %copy-start.6 = (bf16[2,1024,4,64]{1,3,2,0:T(8,128)(2,1)S(1)}, bf16[2,1024,4,64]{1,3,2,0:T(8,128)(2,1)}, u32[]{:S(2)}) copy-start(bf16[2,1024,4,64]{1,3,2,0:T(8,128)(2,1)} %copy-done.5) | copy-start | bytes 3145732 | tf_op jit(solution)/shard_map/while
  289.5 19.6 %copy-start.5 = (bf16[2,1024,4,64]{1,3,2,0:T(8,128)(2,1)}, bf16[2,1024,4,64]{1,3,2,0:T(8,128)(2,1)S(1)}, u32[]{:S(2)}) copy-start(bf16[2,1024,4,64]{1,3,2,0:T(8,128)(2,1)S(1)} %get-tuple-element.479) | copy-start | bytes 3145732 | tf_op jit(solution)/shard_map/while
  292.9 4.7 copy-start.1
  299.9 2.2 copy-start.4
  302.1 4.6 copy-start
  309.1 2.1 copy-start.2
  331.0 3.7 copy-start.3
  361.7 24.2 %copy-start.6 = (bf16[2,1024,4,64]{1,3,2,0:T(8,128)(2,1)S(1)}, bf16[2,1024,4,64]{1,3,2,0:T(8,128)(2,1)}, u32[]{:S(2)}) copy-start(bf16[2,1024,4,64]{1,3,2,0:T(8,128)(2,1)} %copy-done.5) | copy-start | bytes 3145732 | tf_op jit(solution)/shard_map/while
  389.3 9.3 %copy-start.19 = (f32[2048,16]{0,1:T(8,128)S(1)}, f32[2048,16]{0,1:T(8,128)}, u32[]{:S(2)}) copy-start(f32[2048,16]{0,1:T(8,128)} %copy-done.18) | copy-start | bytes 393220
  394.4 5.6 copy-start.21
  398.6 2.5 copy-start.15
  398.6 2.7 copy-start.14
  402.7 2.0 copy-start.41
  403.1 1.6 copy-start.13
  410.0 145.9 %reduce-scatter.12.cloned.1.call-start = ((), (), s32[]{:S(2)}) async-start(), calls=%async_computation.15 | async-start | bytes 5242880 | tf_op jit(solution)/shard_map/reduce_scatter | solution.py:256
  437.5 30.0 %copy-start.40 = (bf16[1024,1024]{1,0:T(8,128)(2,1)S(1)}, bf16[1024,1024]{1,0:T(8,128)(2,1)}, u32[]{:S(2)}) copy-start(bf16[1024,1024]{1,0:T(8,128)(2,1)} %all-gather.14.cloned.1.call-done) | copy-start | bytes 6291460
  465.4 2.0 copy-start.46
  473.8 130.7 %reduce-scatter.8.cloned.1.call-start = ((), (), s32[]{:S(2)}) async-start(), calls=%async_computation.12 | async-start | bytes 5242880 | tf_op jit(solution)/shard_map/reduce_scatter | solution.py:205
  476.7 12.3 %copy-start.39 = (bf16[1024,1024]{1,0:T(8,128)(2,1)S(1)}, bf16[1024,1024]{1,0:T(8,128)(2,1)}, u32[]{:S(2)}) copy-start(bf16[1024,1024]{1,0:T(8,128)(2,1)} %all-gather.16.cloned.1.call-done) | copy-start | bytes 6291460
  489.0 6.4 copy-start.17
  498.7 133.2 %reduce-scatter.16.cloned.1.call-start = ((), (), s32[]{:S(2)}) async-start(), calls=%async_computation.17 | async-start | bytes 1179648 | tf_op jit(solution)/shard_map/reduce_scatter | solution.py:244
  503.3 206.1 %reduce-scatter.14.cloned.1.call-start = ((), (), s32[]{:S(2)}) async-start(), calls=%async_computation.16 | async-start | bytes 3538944 | tf_op jit(solution)/shard_map/reduce_scatter | solution.py:242
  511.7 288.8 %reduce-scatter.20.cloned.1.call-start = ((), (), s32[]{:S(2)}) async-start(), calls=%async_computation.19 | async-start | bytes 4718592 | tf_op jit(solution)/shard_map/reduce_scatter | solution.py:245
  522.1 370.9 %reduce-scatter.18.cloned.1.call-start = ((), (), s32[]{:S(2)}) async-start(), calls=%async_computation.18 | async-start | bytes 4718592 | tf_op jit(solution)/shard_map/reduce_scatter | solution.py:243
  532.6 1.6 copy-start.43
  532.6 1.8 copy-start.44
  532.6 2.0 copy-start.31
  532.7 23.3 %copy-start.7 = (bf16[512,1024]{1,0:T(8,128)(2,1)S(1)}, bf16[512,1024]{1,0:T(8,128)(2,1)}, u32[]{:S(2)}) copy-start(bf16[512,1024]{1,0:T(8,128)(2,1)} %param.19) | copy-start | bytes 3145732
  532.7 23.3 %copy-start.23 = (f32[512]{0:T(512)S(1)}, f32[512]{0:T(512)}, u32[]{:S(2)}) copy-start(f32[512]{0:T(512)} %copy-done.22) | copy-start | bytes 6148
  532.7 23.3 %copy-start.25 = (f32[1024]{0:T(1024)S(1)}, f32[1024]{0:T(1024)}, u32[]{:S(2)}) copy-start(f32[1024]{0:T(1024)} %copy-done.24) | copy-start | bytes 12292
  532.7 23.3 %copy-start.27 = (f32[1024]{0:T(1024)S(1)}, f32[1024]{0:T(1024)}, u32[]{:S(2)}) copy-start(f32[1024]{0:T(1024)} %copy-done.26) | copy-start | bytes 12292
  532.7 25.9 %copy-start.35 = (f32[512]{0:T(512)S(1)}, f32[512]{0:T(512)}, u32[]{:S(2)}) copy-start(f32[512]{0:T(512)} %copy-done.34) | copy-start | bytes 6148
  532.7 25.9 %copy-start.30 = (f32[512]{0:T(512)S(1)}, f32[512]{0:T(512)}, u32[]{:S(2)}) copy-start(f32[512]{0:T(512)} %copy-done.29) | copy-start | bytes 6148
  532.7 29.3 %copy-start.12 = (bf16[512,1024]{1,0:T(8,128)(2,1)S(1)}, bf16[512,1024]{1,0:T(8,128)(2,1)}, u32[]{:S(2)}) copy-start(bf16[512,1024]{1,0:T(8,128)(2,1)} %param.21) | copy-start | bytes 3145732
  532.7 29.3 %copy-start.33 = (f32[512]{0:T(512)S(1)}, f32[512]{0:T(512)}, u32[]{:S(2)}) copy-start(f32[512]{0:T(512)} %copy-done.32) | copy-start | bytes 6148
  555.9 6.1 copy-start.9
  555.9 6.1 copy-start.10
  602.2 291.3 %copy-start.45 = (f32[32]{0:T(128)}, f32[32]{0:T(128)S(1)}, u32[]{:S(2)}) copy-start(f32[32]{0:T(128)S(1)} %dynamic-slice.7) | copy-start | bytes 388
  (4 other events, 3.2 us)
Sparse Core Ops, SparseCore 0:
  10.2 47.2 all-gather.9
  61.1 34.3 all-gather.7
  97.0 34.4 all-gather.17
  133.6 49.2 all-gather.13
  184.9 32.9 all-gather.11
  219.9 49.2 all-gather.15
  410.1 41.0 reduce-scatter.9
  474.0 43.1 reduce-scatter.11
  519.7 44.4 reduce-scatter.7
  568.4 63.4 reduce-scatter.15
  636.1 73.1 reduce-scatter.13
  713.4 87.0 reduce-scatter.19
  805.1 87.8 reduce-scatter.17
where the time goes:
time: 914 us; the launch traced here: 901 us
  waiting for transfers between devices  288 us (32%)
  matrix products  186 us (20%)
  blocking collectives  171 us (19%)
  local copies, waits for them, and re-layouts  168 us (18%)
  other arithmetic  68.2 us (7%)
  between operations  17.2 us (2%)
    unnamed x4, blocking collectives  121 us
    dynamic_update_slice x12, local copies, waits for them, and re-layouts, local(): lax.map(attend_back, (shaped(query), shaped(keys), shaped(values), labels...  115 us
    reduce_scatter x1, waiting for transfers between devices, local(): lax.psum_scatter(expand_grad, 'fsdp', scatter_dimension=0, tiled=True)  92.5 us
    reduce_scatter x1, waiting for transfers between devices, local(): lax.psum_scatter(shrink_grad, 'fsdp', scatter_dimension=0, tiled=True)  91.2 us
    reduce_scatter x1, waiting for transfers between devices, local(): lax.psum_scatter(project_grad, 'fsdp', scatter_dimension=0, tiled=True)  77.4 us
    dot_general x4, matrix products, contract_columns(): lax.dot_general(left, right, (((1,), (1,)), ((), ())), preferred_element_...  44.1 us
    all_gather x1, blocking collectives, local(): lax.all_gather(dense_weight, 'fsdp', axis=0, tiled=True)  33.6 us
    dot_general x4, matrix products, contract_rows(): lax.dot_general(left, right, (((0,), (0,)), ((), ())), preferred_element_...  33.4 us
  transfers between devices with their start and end apart: 13, of which 4 were waited for; matrix products, arithmetic and copies ran while one was open for 46% of the time, Pallas kernels for 0%

commit v1 on v0

--- a/solution.py
+++ b/solution.py
@@ -4,6 +4,7 @@
 import jax.numpy as jnp
 from jax import lax
 from jax.sharding import PartitionSpec as P
+from jax.lax import axis_index, axis_size, ppermute
 
 HD = 64
 ROT = 16
@@ -151,6 +152,41 @@
     shrink_weight,
     shrink_bias,
 ):
+
+    def match_chains(array_dim, axis_tag, view):
+        t1 = axis_size(axis_tag)
+        r1 = axis_index(axis_tag)
+        wide_out, carry_out, v1 = (t1, r1, view.shape[array_dim])
+        so_far_all = []
+        q = 0
+        while q < wide_out:
+            so_far_all.append((q, (q + 1) % wide_out))
+            q += 1
+        gallery = []
+        q = 0
+        while q < wide_out:
+            gallery.append((q, (q - 1) % wide_out))
+            q = q + 1
+        built = jnp.zeros(
+            (*view.shape[:array_dim], wide_out * v1, *view.shape[array_dim + 1 :]), view.dtype
+        )
+        built = lax.dynamic_update_slice_in_dim(built, view, carry_out * v1, axis=array_dim)
+        later = u_next = view
+        next_value = wide_out // 2
+        num = 1
+        while num < next_value + 1:
+            later = ppermute(later, axis_name=axis_tag, perm=so_far_all)
+            built = lax.dynamic_update_slice_in_dim(
+                built, later, (carry_out - num) % wide_out * v1, axis=array_dim
+            )
+            if num < wide_out - next_value:
+                u_next = ppermute(u_next, axis_tag, gallery)
+                built = lax.dynamic_update_slice_in_dim(
+                    built, u_next, (carry_out + num) % wide_out * v1, axis=array_dim
+                )
+            num += 1
+        return built
+
     rank = lax.axis_index("tensor")
     rows = inputs.shape[0]
     group = segments.shape[0]
@@ -167,7 +203,7 @@
     gathered = (
         lax.all_gather(project_weight, "fsdp", axis=0, tiled=True),
         lax.all_gather(expand_weight, "fsdp", axis=0, tiled=True),
-        lax.all_gather(dense_weight, "fsdp", axis=0, tiled=True),
+        match_chains(0, "fsdp", dense_weight),
         lax.all_gather(shrink_weight, "fsdp", axis=0, tiled=True),
         lax.all_gather(project_bias, "fsdp", axis=0, tiled=True),
         lax.all_gather(expand_bias, "fsdp", axis=0, tiled=True),

time: 914 us -> 903 us (0.988)
  blocking collectives: 171 us -> 135 us
  starting transfers between devices: 0.99 us -> 15.4 us
    all_gather x1 -> x0, blocking collectives: 33.6 us -> none  [local(): lax.all_gather(dense_weight, 'fsdp', axis=0, tiled=True)]
    ppermute x0 -> x7, starting transfers between devices: none -> 14.4 us  [the longest x3 10.9 us: match_chains(): u_next = ppermute(u_next, axis_tag, gallery)]
  transfers between devices with their start and end apart: 13 -> 20, of which waited for: 4 -> 7; matrix products, arithmetic and copies ran while one was open for 46% -> 47% of each run, Pallas kernels for 0% -> 0%
where the time goes in v1:
time: 903 us; the launch traced here: 889 us
  waiting for transfers between devices  295 us (33%)
  matrix products  186 us (21%)
  local copies, waits for them, and re-layouts  172 us (19%)
  blocking collectives  135 us (15%)
  other arithmetic  66.4 us (7%)
  between operations  17.4 us (2%)
  starting transfers between devices  15.4 us (2%)
    unnamed x4, blocking collectives  119 us
    dynamic_update_slice x12, local copies, waits for them, and re-layouts, local(): lax.map(attend_back, (shaped(query), shaped(keys), shaped(values), labels...  115 us
    reduce_scatter x1, waiting for transfers between devices, local(): lax.psum_scatter(expand_grad, 'fsdp', scatter_dimension=0, tiled=True)  92.3 us
    reduce_scatter x1, waiting for transfers between devices, local(): lax.psum_scatter(shrink_grad, 'fsdp', scatter_dimension=0, tiled=True)  91.1 us
    reduce_scatter x1, waiting for transfers between devices, local(): lax.psum_scatter(project_grad, 'fsdp', scatter_dimension=0, tiled=True)  77.5 us
    dot_general x4, matrix products, contract_columns(): lax.dot_general(left, right, (((1,), (1,)), ((), ())), preferred_element_...  43.2 us
    dot_general x4, matrix products, contract_rows(): lax.dot_general(left, right, (((0,), (0,)), ((), ())), preferred_element_...  33.5 us
    reduce_scatter x1, waiting for transfers between devices, local(): lax.psum_scatter(dense_grad, 'fsdp', scatter_dimension=0, tiled=True)  24.4 us
  transfers between devices with their start and end apart: 20, of which 7 were waited for; matrix products, arithmetic and copies ran while one was open for 47% of the time, Pallas kernels for 0%

profile of v1, /device:TPU:0, one launch (start us, length us, event | category | flops | bytes accessed | tf_op | source)
XLA Modules:
  0.0 888.8 jit_solution(11332679227281956693)
XLA Ops:
  11.4 42.8 %all-reduce.15 = (f32[1024]{0:T(1024)S(1)}, f32[1024]{0:T(1024)S(1)}, f32[1024]{0:T(1024)S(1)}, f32[1024]{0:T(1024)S(1)}) all-reduce(f32[1024]{0:T(1024)S(1)} %dynamic-update-slice.4, f32[1024]{0:T(1024)S(1)} %dynamic-update-slice.3, f32[1024]{0:T(1024)S(1)} %dynamic-update-slice.1, ...), channel_id=1, replica_groups=mesh['fsdp'=8,'tensor'=4] {'fsdp','tensor'}, use_global_device_ids=true, to_apply=%add.4 | all-reduce | flops 4096 | bytes 32768
  57.9 3.2 fusion.108
  66.1 2.4 collective-permute-start.1
  70.4 18.1 %all-reduce.2 = bf16[768]{0:T(1024)(128)(2,1)S(1)} all-reduce(bf16[768]{0:T(1024)(128)(2,1)S(1)} %dynamic-update-slice.2), channel_id=1, replica_groups=mesh['fsdp'=8,'tensor'=4] {'fsdp'}, use_global_device_ids=true, to_apply=%add.2 | all-reduce | flops 768 | bytes 3072
  91.4 3.7 collective-permute-start.3
  97.7 4.7 collective-permute-start.5
  106.1 5.7 collective-permute-done.6
  112.4 5.8 convolution_add_fusion.1
  122.3 2.5 pad_maximum_fusion.1
  125.3 2.6 concatenate.55
  133.6 37.7 %while.26 = (s32[]{:T(128)}, bf16[2,1024,4,64]{1,3,2,0:T(8,128)(2,1)}, f32[2,4,1024]{2,1,0:T(4,128)S(1)}, bf16[2,1024,4,64]{1,3,2,0:T(8,128)(2,1)}, s32[2,1024]{...) while((s32[]{:T(128)}, ...), condition=%wide.region_7.8_spmd, body=%wide.region_2.7_spmd.sunk | while | flops 1131677184 | bytes 67310776 | solution.py:234
  141.9 2.3 fusion.208
  144.2 3.6 fusion.212
  147.9 3.7 fusion.209
  162.9 3.6 fusion.212
  166.5 3.7 fusion.209
  171.3 3.6 convolution_convert_fusion.2
  176.8 4.1 copy.57
  180.9 193.2 %while.27 = (s32[]{:T(128)}, f32[2,1024,4,64]{1,0,3,2:T(2,128)}, f32[2,1024,4,64]{1,0,3,2:T(2,128)}, bf16[2,1024,4,64]{1,0,3,2:T(2,128)(2,1)}, bf16[2,1024,4,64]...) while((s32[]{:T(128)}, f32[2,1024,4,64]{1,0,3,2:T(2,128)}, ...), condition=%wide.region_12.13_spmd, body=%wide.region_9.12_spmd.sunk | while | flops 2755130880 | bytes 284876160 | solution.py:266
  184.5 4.6 multiply_reduce_fusion.5
  189.1 2.4 multiply_convert_fusion.6
  193.6 4.6 multiply_reduce_fusion.4
  198.3 2.4 multiply_convert_fusion.5
  203.8 18.7 %dynamic_update_slice.68 = f32[2,1024,4,64]{1,0,3,2:T(2,128)} dynamic-update-slice(f32[2,1024,4,64]{1,0,3,2:T(2,128)} %get-tuple-element.462, f32[1,1024,4,64]{1,0,3,2:T(1,128)S(1)} %copy.97, s32[]{:T(128)} %get-tuple-element.460, s32[]{:T(128)} %constant.166.clone.1..sunk.1, s32[]{:T(128)} %constant.166.clone.1..sunk.1, s32[]{:T(128)} %constant.166.clone.1..sunk.1) | dynamic-update-slice | bytes 2097156 | tf_op jit(solution)/shard_map/while/body/jit(dynamic_update_index_in_dim)/dynamic_update_slice | solution.py:266
  222.5 3.7 fusion.230
  228.8 18.7 %dynamic_update_slice.67 = f32[2,1024,4,64]{1,0,3,2:T(2,128)} dynamic-update-slice(f32[2,1024,4,64]{1,0,3,2:T(2,128)} %get-tuple-element.461, f32[1,1024,4,64]{1,0,3,2:T(1,128)S(1)} %copy.96, s32[]{:T(128)} %get-tuple-element.460, s32[]{:T(128)} %constant.166.clone.1..sunk.1, s32[]{:T(128)} %constant.166.clone.1..sunk.1, s32[]{:T(128)} %constant.166.clone.1..sunk.1) | dynamic-update-slice | bytes 2097156 | tf_op jit(solution)/shard_map/while/body/jit(dynamic_update_index_in_dim)/dynamic_update_slice | solution.py:266
  247.4 5.7 fusion.233
  253.2 5.9 fusion.234
  260.0 17.4 %dynamic_update_slice.69 = bf16[2,1024,4,64]{1,0,3,2:T(2,128)(2,1)} dynamic-update-slice(bf16[2,1024,4,64]{1,0,3,2:T(2,128)(2,1)} %get-tuple-element.463, bf16[1,1024,4,64]{1,0,3,2:T(2,128)(2,1)S(1)} %copy.98, s32[]{:T(128)} %get-tuple-element.460, s32[]{:T(128)} %constant.166.clone.1..sunk.1, s32[]{:T(128)} %constant.166.clone.1..sunk.1, s32[]{:T(128)} %constant.166.clone.1..sunk.1) | dynamic-update-slice | bytes 1048580 | tf_op jit(solution)/shard_map/while/body/jit(dynamic_update_index_in_dim)/dynamic_update_slice | solution.py:266
  280.8 4.6 multiply_reduce_fusion.5
  285.4 2.4 multiply_convert_fusion.6
  290.0 4.6 multiply_reduce_fusion.4
  294.6 2.4 multiply_convert_fusion.5
  300.2 18.7 %dynamic_update_slice.68 = f32[2,1024,4,64]{1,0,3,2:T(2,128)} dynamic-update-slice(f32[2,1024,4,64]{1,0,3,2:T(2,128)} %get-tuple-element.462, f32[1,1024,4,64]{1,0,3,2:T(1,128)S(1)} %copy.97, s32[]{:T(128)} %get-tuple-element.460, s32[]{:T(128)} %constant.166.clone.1..sunk.1, s32[]{:T(128)} %constant.166.clone.1..sunk.1, s32[]{:T(128)} %constant.166.clone.1..sunk.1) | dynamic-update-slice | bytes 2097156 | tf_op jit(solution)/shard_map/while/body/jit(dynamic_update_index_in_dim)/dynamic_update_slice | solution.py:266
  318.8 3.7 fusion.230
  325.1 18.7 %dynamic_update_slice.67 = f32[2,1024,4,64]{1,0,3,2:T(2,128)} dynamic-update-slice(f32[2,1024,4,64]{1,0,3,2:T(2,128)} %get-tuple-element.461, f32[1,1024,4,64]{1,0,3,2:T(1,128)S(1)} %copy.96, s32[]{:T(128)} %get-tuple-element.460, s32[]{:T(128)} %constant.166.clone.1..sunk.1, s32[]{:T(128)} %constant.166.clone.1..sunk.1, s32[]{:T(128)} %constant.166.clone.1..sunk.1) | dynamic-update-slice | bytes 2097156 | tf_op jit(solution)/shard_map/while/body/jit(dynamic_update_index_in_dim)/dynamic_update_slice | solution.py:266
  343.8 5.7 fusion.233
  349.5 5.9 fusion.234
  356.3 17.4 %dynamic_update_slice.69 = bf16[2,1024,4,64]{1,0,3,2:T(2,128)(2,1)} dynamic-update-slice(bf16[2,1024,4,64]{1,0,3,2:T(2,128)(2,1)} %get-tuple-element.463, bf16[1,1024,4,64]{1,0,3,2:T(2,128)(2,1)S(1)} %copy.98, s32[]{:T(128)} %get-tuple-element.460, s32[]{:T(128)} %constant.166.clone.1..sunk.1, s32[]{:T(128)} %constant.166.clone.1..sunk.1, s32[]{:T(128)} %constant.166.clone.1..sunk.1) | dynamic-update-slice | bytes 1048580 | tf_op jit(solution)/shard_map/while/body/jit(dynamic_update_index_in_dim)/dynamic_update_slice | solution.py:266
  374.1 3.1 reshape.508
  377.2 4.1 reshape.509
  382.2 2.4 slice.161
  392.6 5.3 convolution_convert_fusion
  398.5 16.1 %all-gather = bf16[8,1,128]{2,1,0:T(2,128)(2,1)S(1)} all-gather(bf16[1,1,128]{2,1,0:T(2,128)(2,1)S(1)} %bitcast.260), channel_id=1, replica_groups=mesh['fsdp'=8,'tensor'=4] {'fsdp'}, dimensions={0}, use_global_device_ids=true | all-gather | bytes 2304 | tf_op jit(solution)/shard_map/all_gather | solution.py:209
  414.7 10.7 %fusion.139 = f32[2048,1024]{1,0:T(8,128)} fusion(bf16[2048,1024]{1,0:T(8,128)(2,1)} %all-gather.12.cloned.1.call-done, bf16[1024,1024]{1,0:T(8,128)(2,1)} %all-gather.14.cloned.1.call-done), kind=kOutput, calls=%fused_computation.253 | convolution fusion | flops 4294967296 | bytes 14680064 | tf_op jit(solution)/shard_map/dot_general | solution.py:236
  425.4 27.9 %convert_reduce_fusion = (f32[1024]{0:T(1024)S(1)}, bf16[2048,1024]{1,0:T(8,128)(2,1)S(1)}, f32[2048,1024]{1,0:T(8,128)}) fusion(f32[2048,1024]{1,0:T(8,128)} %fusion.139, f32[1024]{0:T(1024)S(1)} %bitcast.258, bf16[2048,1024]{1,0:T(8,128)(2,1)} %all-gather.18.cloned.1.call-done, bf16[1024,1024]{1,0:T(8,128)(2,1)} %all-gather.16.cloned.1.call-done), kind=kOutput, calls=%fused_computation.132 | convolution fusion | flops 4452252672 | bytes 27271168 | tf_op jit(solution)/shard_map/dot_general | solution.py:133
  455.3 6.4 convolution_convert_fusion.1
  464.3 12.1 %multiply_convert_fusion.2 = bf16[2048,1024]{1,0:T(8,128)(2,1)} fusion(f32[2048,1024]{1,0:T(8,128)} %get-tuple-element.214, f32[2048,1024]{1,0:T(8,128)} %fusion.139, f32[1024]{0:T(1024)S(1)} %bitcast.259), kind=kLoop, calls=%fused_computation.135 | loop fusion | flops 8388608 | bytes 20975616 | tf_op jit(solution)/shard_map/convert_element_type | solution.py:239
  476.4 6.3 fusion.140
  482.7 4.4 add_convert_fusion.1
  487.2 4.5 fusion.142
  491.7 8.4 fusion.141
  500.4 10.1 %fusion.144 = f32[1024,1024]{1,0:T(8,128)} fusion(bf16[2048,1024]{1,0:T(8,128)(2,1)} %multiply_convert_fusion.2, bf16[2048,1024]{1,0:T(8,128)(2,1)} %all-gather.18.cloned.1.call-done), kind=kOutput, calls=%fused_computation.258 | convolution fusion | flops 4294967296 | bytes 12582912 | tf_op jit(solution)/shard_map/dot_general | solution.py:127
  510.6 10.6 %fusion.143 = f32[1024,1024]{1,0:T(8,128)} fusion(bf16[2048,1024]{1,0:T(8,128)(2,1)} %all-gather.12.cloned.1.call-done, bf16[2048,1024]{1,0:T(8,128)(2,1)} %copy-done.47), kind=kOutput, calls=%fused_computation.257 | convolution fusion | flops 4294967296 | bytes 12582912 | tf_op jit(solution)/shard_map/dot_general | solution.py:127
  523.3 19.9 %all-reduce.16 = (f32[768]{0:T(1024)S(1)}, f32[1024]{0:T(1024)S(1)}) all-reduce(f32[768]{0:T(1024)S(1)} %reduce_sum.174, f32[1024]{0:T(1024)S(1)} %get-tuple-element.212), channel_id=10, replica_groups=mesh['fsdp'=8,'tensor'=4] {'fsdp'}, use_global_device_ids=true, to_apply=%region_29.30.clone | all-reduce | flops 1792 | bytes 14336
  544.5 2.7 fusion.112
  547.1 3.4 fusion.118
  550.6 2.6 add_convert_fusion.2
  553.1 37.7 %all-reduce.14 = (f32[1024]{0:T(1024)S(1)}, f32[1024]{0:T(1024)S(1)}, f32[1024]{0:T(1024)S(1)}, f32[1024]{0:T(1024)S(1)}, f32[1024]{0:T(1024)S(1)}, /*index=5*/f32[1024]{0:T(1024)S(1)}, f32[1024]{0:T(1024)S(1)}) all-reduce(f32[1024]{0:T(1024)S(1)} %dynamic-update-slice.6, ...), channel_id=1, replica_groups=mesh['fsdp'=8,'tensor'=4] {'fsdp','tensor'}, use_global_device_ids=true, to_apply=%add.6 | all-reduce | flops 7168 | bytes 57344
  593.3 2.6 fusion.116
  595.9 24.4 %reduce-scatter.16.cloned.1.call-done = f32[32,1024]{1,0:T(8,128)} async-done(((f32[256,1024]{1,0:T(8,128)}), f32[32,1024]{1,0:T(8,128)}) %reduce-scatter.16.cloned.1.call-update) | async-done | bytes 131088 | tf_op jit(solution)/shard_map/reduce_scatter | solution.py:280
  620.3 77.5 %reduce-scatter.14.cloned.1.call-done = f32[128,768]{1,0:T(8,128)} async-done(((f32[1024,768]{1,0:T(8,128)}), f32[128,768]{1,0:T(8,128)}) %reduce-scatter.14.cloned.1.call-update) | async-done | bytes 393232 | tf_op jit(solution)/shard_map/reduce_scatter | solution.py:278
  697.9 91.1 %reduce-scatter.20.cloned.1.call-done = f32[128,1024]{1,0:T(8,128)} async-done(((f32[1024,1024]{1,0:T(8,128)}), f32[128,1024]{1,0:T(8,128)}) %reduce-scatter.20.cloned.1.call-update) | async-done | bytes 524304 | tf_op jit(solution)/shard_map/reduce_scatter | solution.py:281
  788.9 92.3 %reduce-scatter.18.cloned.1.call-done = f32[128,1024]{1,0:T(8,128)} async-done(((f32[1024,1024]{1,0:T(8,128)}), f32[128,1024]{1,0:T(8,128)}) %reduce-scatter.18.cloned.1.call-update) | async-done | bytes 524304 | tf_op jit(solution)/shard_map/reduce_scatter | solution.py:279
  (303 shorter events, 98.7 us)
Async XLA Ops:
  7.2 54.0 %copy-start.37 = (s32[2048]{0:T(1024)S(1)}, s32[2048]{0:T(1024)}, u32[]{:S(2)}) copy-start(s32[2048]{0:T(1024)} %param.20) | copy-start | bytes 24580
  7.2 54.1 %copy-start.11 = (bf16[512,1024]{1,0:T(8,128)(2,1)S(1)}, bf16[512,1024]{1,0:T(8,128)(2,1)}, u32[]{:S(2)}) copy-start(bf16[512,1024]{1,0:T(8,128)(2,1)} %param.21) | copy-start | bytes 3145732
  7.2 105.2 %all-gather.10.cloned.1.call-start = ((), (), s32[]{:S(2)}) async-start(), calls=%async_computation.8 | async-start | bytes 1769472 | tf_op jit(solution)/shard_map/all_gather | solution.py:204
  7.9 104.5 %all-gather.8.cloned.1.call-start = ((), (), s32[]{:S(2)}) async-start(), calls=%async_computation.7 | async-start | bytes 5242880 | tf_op jit(solution)/shard_map/all_gather | solution.py:216
  54.2 8.3 copy-start.25
  54.2 8.3 copy-start.27
  55.7 2.2 copy-start.23
  57.3 6.4 copy-start.30
  57.9 5.9 copy-start.29
  57.9 10.9 %copy-start.38 = (u32[32]{0:T(128)S(1)}, u32[32]{0:T(128)}, u32[]{:S(2)}) copy-start(u32[32]{0:T(128)} %constant.231) | copy-start | bytes 388
  57.9 12.2 %copy-start.43 = (bf16[96]{0:T(256)(128)(2,1)S(1)}, bf16[96]{0:T(256)(128)(2,1)}, u32[]{:S(2)}) copy-start(bf16[96]{0:T(256)(128)(2,1)} %param.27) | copy-start | bytes 580
  61.1 110.2 %all-gather.18.cloned.1.call-start = ((), (), s32[]{:S(2)}) async-start(), calls=%async_computation.13 | async-start | bytes 5242880 | tf_op jit(solution)/shard_map/all_gather | solution.py:253
  61.3 27.2 %copy-start.33 = (f32[512]{0:T(512)}, f32[512]{0:T(512)S(1)}, u32[]{:S(2)}) copy-start(f32[512]{0:T(512)S(1)} %fusion.131) | copy-start | bytes 6148
  62.5 352.1 %all-gather.14.cloned.1.call-start = ((), (), s32[]{:S(2)}) async-start(), calls=%async_computation.10 | async-start | bytes 2359296 | tf_op jit(solution)/shard_map/all_gather | solution.py:205
  63.1 351.5 %all-gather.12.cloned.1.call-start = ((), (), s32[]{:S(2)}) async-start(), calls=%async_computation.9 | async-start | bytes 5242880 | tf_op jit(solution)/shard_map/all_gather | solution.py:217
  63.7 361.6 %all-gather.16.cloned.1.call-start = ((), (), s32[]{:S(2)}) async-start(), calls=%async_computation.11 | async-start | bytes 2359296 | tf_op jit(solution)/shard_map/all_gather | solution.py:207
  63.8 26.6 %collective-permute-start = (bf16[32,1024]{1,0:T(8,128)(2,1)S(1)}, bf16[32,1024]{1,0:T(8,128)(2,1)S(1)}, u32[]{:S(2)}, u32[]{:S(2)}) collective-permute-start(bf16[32,1024]{1,0:T(8,128)(2,1)S(1)} %copy-done.29), channel_id=1, source_target_pairs={{0,4},{4,8},{8,12},{12,16},{16,20},{20,24},{24,28},{28,0},{1,5},{5... | collective-permute-start | bytes 196616 | tf_op jit(solution)/shard_map/ppermute | solution.py:178
  66.1 25.3 %collective-permute-start.1 = (bf16[32,1024]{1,0:T(8,128)(2,1)S(1)}, bf16[32,1024]{1,0:T(8,128)(2,1)S(1)}, u32[]{:S(2)}, u32[]{:S(2)}) collective-permute-start(bf16[32,1024]{1,0:T(8,128)(2,1)S(1)} %copy-done.29), channel_id=1, source_target_pairs={{0,28},{4,0},{8,4},{12,8},{16,12},{20,16},{24,20},{28,24},{1,29},{... | collective-permute-start | bytes 196616 | tf_op jit(solution)/shard_map/ppermute | solution.py:183
  68.6 475.8 %reduce-scatter.10.cloned.1.call-start = ((), (), s32[]{:S(2)}) async-start(), calls=%async_computation.14 | async-start | bytes 5242880 | tf_op jit(solution)/shard_map/reduce_scatter | solution.py:289
  88.8 31.7 %copy-start.16 = (f32[2048,16]{0,1:T(8,128)}, f32[2048,16]{0,1:T(8,128)S(1)}, u32[]{:S(2)}) copy-start(f32[2048,16]{0,1:T(8,128)S(1)} %get-tuple-element.268) | copy-start | bytes 393220
  88.8 31.7 %copy-start.18 = (f32[2048,16]{0,1:T(8,128)}, f32[2048,16]{0,1:T(8,128)S(1)}, u32[]{:S(2)}) copy-start(f32[2048,16]{0,1:T(8,128)S(1)} %get-tuple-element.267) | copy-start | bytes 393220
  90.4 7.3 collective-permute-start.2
  91.4 6.2 collective-permute-start.3
  97.6 7.0 collective-permute-start.4
  97.7 7.8 collective-permute-start.5
  104.6 7.2 collective-permute-start.6
  147.9 3.7 copy-start.20
  166.5 3.7 copy-start.20
  181.0 19.6 %copy-start.5 = (bf16[2,1024,4,64]{1,3,2,0:T(8,128)(2,1)}, bf16[2,1024,4,64]{1,3,2,0:T(8,128)(2,1)S(1)}, u32[]{:S(2)}) copy-start(bf16[2,1024,4,64]{1,3,2,0:T(8,128)(2,1)S(1)} %get-tuple-element.479) | copy-start | bytes 3145732 | tf_op jit(solution)/shard_map/while
  184.4 4.7 copy-start.1
  191.5 2.2 copy-start.4
  193.6 4.6 copy-start
  200.7 2.0 copy-start.2
  222.5 3.7 copy-start.3
  253.2 24.2 %copy-start.6 = (bf16[2,1024,4,64]{1,3,2,0:T(8,128)(2,1)S(1)}, bf16[2,1024,4,64]{1,3,2,0:T(8,128)(2,1)}, u32[]{:S(2)}) copy-start(bf16[2,1024,4,64]{1,3,2,0:T(8,128)(2,1)} %copy-done.5) | copy-start | bytes 3145732 | tf_op jit(solution)/shard_map/while
  277.4 19.6 %copy-start.5 = (bf16[2,1024,4,64]{1,3,2,0:T(8,128)(2,1)}, bf16[2,1024,4,64]{1,3,2,0:T(8,128)(2,1)S(1)}, u32[]{:S(2)}) copy-start(bf16[2,1024,4,64]{1,3,2,0:T(8,128)(2,1)S(1)} %get-tuple-element.479) | copy-start | bytes 3145732 | tf_op jit(solution)/shard_map/while
  280.8 4.7 copy-start.1
  287.8 2.2 copy-start.4
  290.0 4.6 copy-start
  318.8 3.7 copy-start.3
  349.5 24.2 %copy-start.6 = (bf16[2,1024,4,64]{1,3,2,0:T(8,128)(2,1)S(1)}, bf16[2,1024,4,64]{1,3,2,0:T(8,128)(2,1)}, u32[]{:S(2)}) copy-start(bf16[2,1024,4,64]{1,3,2,0:T(8,128)(2,1)} %copy-done.5) | copy-start | bytes 3145732 | tf_op jit(solution)/shard_map/while
  377.1 9.3 %copy-start.17 = (f32[2048,16]{0,1:T(8,128)S(1)}, f32[2048,16]{0,1:T(8,128)}, u32[]{:S(2)}) copy-start(f32[2048,16]{0,1:T(8,128)} %copy-done.16) | copy-start | bytes 393220
  382.2 5.6 copy-start.19
  386.5 2.5 copy-start.15
  386.5 2.7 copy-start.14
  397.9 146.6 %reduce-scatter.12.cloned.1.call-start = ((), (), s32[]{:S(2)}) async-start(), calls=%async_computation.15 | async-start | bytes 5242880 | tf_op jit(solution)/shard_map/reduce_scatter | solution.py:292
  425.4 29.9 %copy-start.40 = (bf16[1024,1024]{1,0:T(8,128)(2,1)S(1)}, bf16[1024,1024]{1,0:T(8,128)(2,1)}, u32[]{:S(2)}) copy-start(bf16[1024,1024]{1,0:T(8,128)(2,1)} %all-gather.14.cloned.1.call-done) | copy-start | bytes 6291460
  461.7 131.5 %reduce-scatter.8.cloned.1.call-start = ((), (), s32[]{:S(2)}) async-start(), calls=%async_computation.12 | async-start | bytes 5242880 | tf_op jit(solution)/shard_map/reduce_scatter | solution.py:241
  464.3 12.2 %copy-start.41 = (bf16[1024,1024]{1,0:T(8,128)(2,1)S(1)}, bf16[1024,1024]{1,0:T(8,128)(2,1)}, u32[]{:S(2)}) copy-start(bf16[1024,1024]{1,0:T(8,128)(2,1)} %all-gather.16.cloned.1.call-done) | copy-start | bytes 6291460
  487.1 133.2 %reduce-scatter.16.cloned.1.call-start = ((), (), s32[]{:S(2)}) async-start(), calls=%async_computation.17 | async-start | bytes 1179648 | tf_op jit(solution)/shard_map/reduce_scatter | solution.py:280
  491.7 206.2 %reduce-scatter.14.cloned.1.call-start = ((), (), s32[]{:S(2)}) async-start(), calls=%async_computation.16 | async-start | bytes 3538944 | tf_op jit(solution)/shard_map/reduce_scatter | solution.py:278
  500.1 288.8 %reduce-scatter.20.cloned.1.call-start = ((), (), s32[]{:S(2)}) async-start(), calls=%async_computation.19 | async-start | bytes 4718592 | tf_op jit(solution)/shard_map/reduce_scatter | solution.py:281
  510.5 370.7 %reduce-scatter.18.cloned.1.call-start = ((), (), s32[]{:S(2)}) async-start(), calls=%async_computation.18 | async-start | bytes 4718592 | tf_op jit(solution)/shard_map/reduce_scatter | solution.py:279
  521.2 23.2 %copy-start.7 = (bf16[512,1024]{1,0:T(8,128)(2,1)S(1)}, bf16[512,1024]{1,0:T(8,128)(2,1)}, u32[]{:S(2)}) copy-start(bf16[512,1024]{1,0:T(8,128)(2,1)} %param.19) | copy-start | bytes 3145732
  521.2 23.2 %copy-start.24 = (f32[512]{0:T(512)S(1)}, f32[512]{0:T(512)}, u32[]{:S(2)}) copy-start(f32[512]{0:T(512)} %copy-done.23) | copy-start | bytes 6148
  521.2 23.2 %copy-start.26 = (f32[1024]{0:T(1024)S(1)}, f32[1024]{0:T(1024)}, u32[]{:S(2)}) copy-start(f32[1024]{0:T(1024)} %copy-done.25) | copy-start | bytes 12292
  521.2 23.2 %copy-start.28 = (f32[1024]{0:T(1024)S(1)}, f32[1024]{0:T(1024)}, u32[]{:S(2)}) copy-start(f32[1024]{0:T(1024)} %copy-done.27) | copy-start | bytes 12292
  521.2 25.9 %copy-start.36 = (f32[512]{0:T(512)S(1)}, f32[512]{0:T(512)}, u32[]{:S(2)}) copy-start(f32[512]{0:T(512)} %copy-done.35) | copy-start | bytes 6148
  521.2 25.9 %copy-start.31 = (f32[512]{0:T(512)S(1)}, f32[512]{0:T(512)}, u32[]{:S(2)}) copy-start(f32[512]{0:T(512)} %copy-done.30) | copy-start | bytes 6148
  521.3 29.3 %copy-start.12 = (bf16[512,1024]{1,0:T(8,128)(2,1)S(1)}, bf16[512,1024]{1,0:T(8,128)(2,1)}, u32[]{:S(2)}) copy-start(bf16[512,1024]{1,0:T(8,128)(2,1)} %param.21) | copy-start | bytes 3145732
  521.3 29.3 %copy-start.34 = (f32[512]{0:T(512)S(1)}, f32[512]{0:T(512)}, u32[]{:S(2)}) copy-start(f32[512]{0:T(512)} %copy-done.33) | copy-start | bytes 6148
  544.4 6.1 copy-start.9
  544.5 6.1 copy-start.10
  590.9 290.8 %copy-start.46 = (f32[32]{0:T(128)}, f32[32]{0:T(128)S(1)}, u32[]{:S(2)}) copy-start(f32[32]{0:T(128)S(1)} %dynamic-slice.7) | copy-start | bytes 388
  (14 other events, 20.2 us)
Sparse Core Ops, SparseCore 0:
  10.2 47.2 all-gather.9
  61.3 34.1 all-gather.7
  97.0 34.4 all-gather.17
  133.5 49.4 all-gather.13
  185.0 32.9 all-gather.11
  220.0 49.5 all-gather.15
  398.0 41.4 reduce-scatter.9
  461.8 43.6 reduce-scatter.11
  508.0 44.4 reduce-scatter.7
  556.8 63.4 reduce-scatter.15
  624.5 73.3 reduce-scatter.13
  701.9 86.9 reduce-scatter.19
  793.6 87.6 reduce-scatter.17
